TPU v7x, 32 devices: a whole 2x2x4 slice. The times are simulated.
32 devices in a mesh: seq: 4 (over y, x), head: 4 (over z), rep: 2 (over core).
Axes of the slice: x: 2, y: 2, z: 4, core: 2. Of those that a mesh axis runs over, the one named last changes fastest.
Arguments:
- query_heads: bfloat16 [2, 8192, 4096], P('rep', 'seq', 'head'), may hold values from -0.59765625 to 0.59765625
- key_heads: bfloat16 [2, 8192, 4096], P('rep', 'seq', 'head'), may hold values from -0.59765625 to 0.59765625
- value_heads: bfloat16 [2, 8192, 4096], P('rep', 'seq', 'head'), may hold values from -6 to 6
- out_cotangent: bfloat16 [2, 8192, 4096], P('rep', 'seq', 'head'), may hold values from -0.19921875 to 0.19921875
- out_weight: bfloat16 [4096, 4096], P('head'), may hold values from -0.09375 to 0.09375
- doc_ends: int32 [2, 7], P('rep'), may hold values from 1 to 8192, as said below
Outputs:
- grad_query: bfloat16 [2, 8192, 4096], P('rep', 'seq', 'head')
- grad_key: bfloat16 [2, 8192, 4096], P('rep', 'seq', 'head')
- grad_value: bfloat16 [2, 8192, 4096], P('rep', 'seq', 'head')
- grad_weight: float32 [4096, 4096], P('head', ('seq', 'rep'))
Inputs may be any that keep to these rules, and one draw needn't show every extreme that they name: `doc_ends`: each row holds 7 strictly increasing document end offsets; its last entry is 8192.
All inputs are finite; a program needn't handle non-finite values.
Results may differ from a plain program's by a relative error of at most 0.0052.
Values may be sent and summed in bfloat16 or wider, within the bound.
No kernel may reach another device: no remote copies, remote signals or barrier semaphores. Data moves between devices by JAX's collectives and lax.ppermute only.
A program may use at most 320 MiB of HBM per device.

v0:
```python
import jax
import jax.numpy as jnp
from jax import lax
from jax.sharding import PartitionSpec as P

HD = 128
BLOCK = 512
highest = lax.Precision.HIGHEST


def prefix(shard, axis, combine, identity, reverse):
    count, here = (lax.axis_size(axis), lax.axis_index(axis))
    everything = jax.tree.map(lambda part: lax.all_gather(part, axis), shard)
    start = jax.tree.map(
        lambda part, zero: jnp.broadcast_to(jnp.asarray(zero, part.dtype), part.shape),
        shard,
        identity,
    )

    def step(k, before):
        at = count - 1 - k if reverse else k
        reached = at > here if reverse else at < here
        new = combine(before, jax.tree.map(lambda part: part[at], everything))
        return jax.tree.map(lambda a, b: jnp.where(reached, a, b), new, before)

    return lax.fori_loop(0, count, step, start)


def doc_counts(positions, ends_row):
    return jnp.sum((ends_row[None, :] <= positions[:, None]).astype(jnp.int32), axis=1)


def local_pass(queries, keys, values, grads, counts, count_before):
    length, heads, width = queries.shape
    blocks = length // BLOCK
    query_blocks = queries.reshape(blocks, BLOCK, heads, width)
    key_blocks = keys.reshape(blocks, BLOCK, heads, width)
    value_blocks = values.reshape(blocks, BLOCK, heads, width)
    grad_blocks = grads.reshape(blocks, BLOCK, heads, width)
    count_blocks = counts.reshape(blocks, BLOCK)
    before_each = jnp.concatenate([jnp.reshape(count_before, (1,)), count_blocks[:-1, -1]])
    last_each = count_blocks[:, -1]
    rows = lax.broadcasted_iota(jnp.int32, (BLOCK, BLOCK), 0)
    cols = lax.broadcasted_iota(jnp.int32, (BLOCK, BLOCK), 1)
    allowed = (
        (count_blocks[:, :, None] == count_blocks[:, None, :]) & (rows >= cols)[None]
    ).astype(jnp.float32)
    scores = jnp.einsum(
        "nthe,nshe->nhts", query_blocks, key_blocks, preferred_element_type=jnp.float32
    )
    attn = (scores * allowed[:, None]).astype(jnp.bfloat16)
    back = jnp.einsum(
        "nthe,nshe->nhts", grad_blocks, value_blocks, preferred_element_type=jnp.float32
    )
    pgrad = (back * allowed[:, None]).astype(jnp.bfloat16)
    out_intra = jnp.einsum(
        "nhts,nshe->nthe", attn, value_blocks, preferred_element_type=jnp.float32
    )
    dq_intra = jnp.einsum("nhts,nshe->nthe", pgrad, key_blocks, preferred_element_type=jnp.float32)
    dk_intra = jnp.einsum(
        "nhts,nthe->nshe", pgrad, query_blocks, preferred_element_type=jnp.float32
    )
    dv_intra = jnp.einsum("nhts,nthe->nshe", attn, grad_blocks, preferred_element_type=jnp.float32)
    first_match = (count_blocks == before_each[:, None])[:, :, None, None]
    last_match = (count_blocks == last_each[:, None])[:, :, None, None]
    keep = (last_each == before_each).astype(jnp.float32)
    tails = jnp.einsum(
        "nshe,nshf->nhef",
        key_blocks * last_match.astype(jnp.bfloat16),
        value_blocks,
        preferred_element_type=jnp.float32,
    )
    head_sums = jnp.einsum(
        "nthe,nthf->nhef",
        query_blocks * first_match.astype(jnp.bfloat16),
        grad_blocks,
        preferred_element_type=jnp.float32,
    )

    def link_step(state, item):
        return (item[0] + item[1] * state, state)

    empty = jnp.zeros((heads, width, width), jnp.float32)
    final_tail, states_before = lax.scan(link_step, empty, (tails, keep))
    final_head, states_after = lax.scan(link_step, empty, (head_sums, keep), reverse=True)
    first_weight = first_match.astype(jnp.float32)
    last_weight = last_match.astype(jnp.float32)
    outputs = out_intra + first_weight * jnp.einsum(
        "nthe,nhef->nthf", query_blocks.astype(jnp.float32), states_before, precision=highest
    )
    dq = dq_intra + first_weight * jnp.einsum(
        "nthf,nhef->nthe", grad_blocks.astype(jnp.float32), states_before, precision=highest
    )
    dk = dk_intra + last_weight * jnp.einsum(
        "nshf,nhef->nshe", value_blocks.astype(jnp.float32), states_after, precision=highest
    )
    dv = dv_intra + last_weight * jnp.einsum(
        "nshe,nhef->nshf", key_blocks.astype(jnp.float32), states_after, precision=highest
    )
    shape = (length, heads, width)
    return (
        outputs.reshape(shape),
        dq.reshape(shape),
        dk.reshape(shape),
        dv.reshape(shape),
        final_tail,
        final_head,
    )


def link_states(earlier, later):
    return (jnp.maximum(earlier[0], later[0]), later[1] + (1.0 - later[0]) * earlier[1])


def on_device(query_heads, key_heads, value_heads, out_cotangent, out_weight, doc_ends):
    length = query_heads.shape[1]
    heads = query_heads.shape[2] // HD
    queries = query_heads[0].reshape(length, heads, HD)
    keys = key_heads[0].reshape(length, heads, HD)
    values = value_heads[0].reshape(length, heads, HD)
    full_cotangent = lax.all_gather(out_cotangent, "head", axis=2, tiled=True)[0]
    grads_flat = lax.dot_general(
        full_cotangent, out_weight, (((1,), (1,)), ((), ())), preferred_element_type=jnp.float32
    ).astype(jnp.bfloat16)
    grads = grads_flat.reshape(length, heads, HD)
    offset = lax.axis_index("seq") * length
    positions = offset + jnp.arange(length, dtype=jnp.int32)
    ends_row = doc_ends[0]
    counts = doc_counts(positions, ends_row)
    count_before = doc_counts(jnp.reshape(offset - 1, (1,)), ends_row)[0]
    outputs, dq, dk, dv, tail, head = local_pass(queries, keys, values, grads, counts, count_before)
    flag = (counts[-1] != count_before).astype(jnp.float32)
    identity = (jnp.zeros((), jnp.float32), jnp.zeros_like(tail))
    flag_before, carry_before = prefix((flag, tail), "seq", link_states, identity, False)
    flag_after, carry_after = prefix((flag, head), "seq", link_states, identity, True)
    entry_weight = (counts == count_before).astype(jnp.float32)[:, None, None]
    exit_weight = (counts == counts[-1]).astype(jnp.float32)[:, None, None]
    outputs = outputs + entry_weight * jnp.einsum(
        "the,hef->thf", queries.astype(jnp.float32), carry_before, precision=highest
    )
    dq = dq + entry_weight * jnp.einsum(
        "thf,hef->the", grads.astype(jnp.float32), carry_before, precision=highest
    )
    dk = dk + exit_weight * jnp.einsum(
        "thf,hef->the", values.astype(jnp.float32), carry_after, precision=highest
    )
    dv = dv + exit_weight * jnp.einsum(
        "the,hef->thf", keys.astype(jnp.float32), carry_after, precision=highest
    )
    flat = heads * HD
    attention_out = outputs.reshape(length, flat).astype(jnp.bfloat16)
    grad_query = dq.reshape(1, length, flat).astype(jnp.bfloat16)
    grad_key = dk.reshape(1, length, flat).astype(jnp.bfloat16)
    grad_value = dv.reshape(1, length, flat).astype(jnp.bfloat16)
    partial_grad = lax.dot_general(
        attention_out, full_cotangent, (((0,), (0,)), ((), ())), preferred_element_type=jnp.float32
    )
    summed = lax.psum(partial_grad, ("seq", "rep"))
    columns = summed.shape[1] // lax.axis_size(("seq", "rep"))
    grad_weight = lax.dynamic_slice_in_dim(
        summed, lax.axis_index(("seq", "rep")) * columns, columns, 1
    )
    return (grad_query, grad_key, grad_value, grad_weight)


def solution(mesh):
    in_specs = (
        P("rep", "seq", "head"),
        P("rep", "seq", "head"),
        P("rep", "seq", "head"),
        P("rep", "seq", "head"),
        P("head", None),
        P("rep", None),
    )
    out_specs = (
        P("rep", "seq", "head"),
        P("rep", "seq", "head"),
        P("rep", "seq", "head"),
        P("head", ("seq", "rep")),
    )
    return jax.shard_map(
        on_device, mesh=mesh, in_specs=in_specs, out_specs=out_specs, check_vma=False
    )
```

profile of v0, /device:TPU:0, one launch (start us, length us, event | category | flops | bytes accessed | tf_op | source)
XLA Modules:
  0.0 711.5 jit_solution(5314023280602779764)
XLA Ops:
  33.0 10.0 %while.60 = (s32[]{:T(128)}, f32[8,128,128]{2,1,0:T(8,128)S(1)}, f32[4,8,128,128]{3,2,1,0:T(8,128)S(1)}, f32[4,8,128,128]{3,2,1,0:T(8,128)}, f32[4]{0:T(128)S(1)}, /*index=5*/s32[]{:T(128)}, s32[]{:T(128)}) while((s32[]{:T(128)}, f32[8,128,128]{2,1,0:T(8,128)S(1)}, f32[4,8,128,128]{3,2,1,0:T(8,128)S(1)}, ...), condition=%wide.region_3.4_spmd.clone, body=%wide.region_2.3_spmd.clone.sunk | while | flops 524291 | bytes 2621560 | solution.py:84
  48.1 11.7 %all-reduce = f32[4]{0:T(128)S(1)} all-reduce(f32[4]{0:T(128)S(1)} %dynamic-update-slice), channel_id=1, replica_groups=mesh['seq'=4,'head'=4,'rep'=2] {'seq'}, use_global_device_ids=true, to_apply=%add | all-reduce | flops 4 | bytes 32
  75.2 11.6 %multiply_convert_fusion = bf16[4,8,512,512]{3,2,1,0:T(8,128)(2,1)} fusion(f32[4,512,512]{2,1,0:T(8,128)} %and_convert_fusion, bf16[4,512,8,128]{1,3,2,0:T(8,128)(2,1)} %copy.184, bf16[4,512,8,128]{1,3,2,0:T(8,128)(2,1)} %copy.175), kind=kOutput, calls=%fused_computation.8 | convolution fusion | flops 2164260864 | bytes 29360128 | tf_op jit(solution)/shard_map/nthe,nshe->nhts/dot_general | solution.py:48
  86.8 17.2 %fusion.24 = f32[4,8,512,128]{3,2,1,0:T(8,128)} fusion(bf16[4,8,512,512]{3,2,1,0:T(8,128)(2,1)} %multiply_convert_fusion, bf16[4,512,8,128]{3,2,1,0:T(8,128)(2,1)} %bitcast.138), kind=kOutput, calls=%fused_computation.39 | convolution fusion | flops 2147483648 | bytes 29360128 | tf_op jit(solution)/shard_map/nhts,nshe->nthe/dot_general | solution.py:56
  104.0 8.4 %bitcast_add_fusion.5 = f32[4,512,8,128]{3,1,2,0:T(8,128)S(1)} fusion(f32[4,8,512,128]{3,2,1,0:T(8,128)} %fusion.24, f32[4,512]{1,0:T(4,128)S(1)} %convert_element_type.133, f32[4,8,128,128]{3,2,1,0:T(8,128)S(1)} %copy-done.4, bf16[4,512,8,128]{1,3,2,0:T(8,128)(2,1)} %copy.184), kind=kOutput, calls=%fused_computation.16 | convolution fusion | flops 3225419776 | bytes 23076864 | tf_op jit(solution)/shard_map/nthe,nhef->nthf/dot_general | solution.py:88
  112.4 8.1 %copy.206 = f32[4,512,8,128]{3,2,1,0:T(8,128)} copy(f32[4,512,8,128]{3,1,2,0:T(8,128)S(1)} %bitcast_add_fusion.5) | data formatting | bytes 16777216 | tf_op jit(solution)/shard_map/add | solution.py:88
  120.5 9.4 %copy.209 = f32[2048,8,128]{0,2,1:T(8,128)} copy(f32[2048,8,128]{2,1,0:T(8,128)} %bitcast.146) | data formatting | bytes 16777216 | tf_op jit(solution)/shard_map/reshape | solution.py:102
  131.8 11.0 %while.61 = (s32[]{:T(128)}, f32[8,128,128]{2,1,0:T(8,128)S(1)}, s32[]{:T(128)}, f32[4,8,128,128]{3,2,1,0:T(8,128)}, f32[4]{0:T(128)S(1)}, /*index=5*/s32[]{:T(128)}, f32[1]{0:T(128)}, s32[]{:T(128)}) while((s32[]{:T(128)}, f32[8,128,128]{2,1,0:T(8,128)S(1)}, s32[]{:T(128)}, f32[4,8,128,128]{3,2,1,0:T(8,128)}, f32[4]{0:T(128)S(1)}, ...), condition=%wide.region_5.6_spmd.clone, body=%wide.region_4.5_spmd.clone.sunk | while | flops 524293 | bytes 1573009 | solution.py:26
  142.8 10.8 %fusion.6 = bf16[2048,8,128]{0,2,1:T(8,128)(2,1)} fusion(f32[2048,8,128]{0,2,1:T(8,128)} %copy.209, f32[8,128,128]{2,1,0:T(8,128)S(1)} %get-tuple-element.364, bf16[2048,8,128]{2,1,0:T(8,128)(2,1)} %bitcast.145, f32[2048]{0:T(1024)S(1)} %get-tuple-element.507), kind=kOutput, calls=%fused_computation.15 | convolution fusion | flops 3227516928 | bytes 17309696 | tf_op jit(solution)/shard_map/the,hef->thf/dot_general | solution.py:138
  153.6 216.7 %all-gather.6.cloned.1.call-done = bf16[1,2048,4096]{2,1,0:T(8,128)(2,1)} async-done(((bf16[1,2048,1024]{2,1,0:T(8,128)(2,1)}), bf16[1,2048,4096]{2,1,0:T(8,128)(2,1)}) %all-gather.6.cloned.1.call-update) | async-done | bytes 16777232 | tf_op jit(solution)/shard_map/all_gather | solution.py:121
  370.3 24.1 %fusion.17 = bf16[2048,1024]{0,1:T(8,128)(2,1)} fusion(bf16[1024,4096]{1,0:T(8,128)(2,1)} %param.18, bf16[1,2048,4096]{2,1,0:T(8,128)(2,1)} %all-gather.6.cloned.1.call-done), kind=kOutput, calls=%fused_computation.34 | convolution fusion | flops 17181966336 | bytes 29360128 | tf_op jit(solution)/shard_map/dot_general | solution.py:122
  394.4 7.8 %reshape_reshape.3 = bf16[4,512,8,128]{1,0,3,2:T(4,128)(2,1)} reshape(bf16[2048,1024]{0,1:T(8,128)(2,1)} %fusion.17) | data formatting | bytes 8388608 | tf_op jit(solution)/shard_map/reshape;reshape | solution.py:39
  402.2 11.6 %multiply_convert_fusion.1 = bf16[4,8,512,512]{3,2,1,0:T(8,128)(2,1)} fusion(f32[4,512,512]{2,1,0:T(8,128)} %and_convert_fusion, bf16[4,512,8,128]{1,0,3,2:T(4,128)(2,1)} %reshape_reshape.3, bf16[4,512,8,128]{3,2,1,0:T(8,128)(2,1)} %bitcast.139), kind=kOutput, calls=%fused_computation.9 | convolution fusion | flops 2164260864 | bytes 29360128 | tf_op jit(solution)/shard_map/nthe,nshe->nhts/dot_general | solution.py:52
  413.9 14.7 %fusion.34 = f32[4,8,512,128]{3,2,1,0:T(8,128)} fusion(bf16[4,8,512,512]{3,2,1,0:T(8,128)(2,1)} %multiply_convert_fusion.1, bf16[4,512,8,128]{1,3,2,0:T(8,128)(2,1)} %copy.175), kind=kOutput, calls=%fused_computation.62 | convolution fusion | flops 2147483648 | bytes 29360128 | tf_op jit(solution)/shard_map/nhts,nshe->nthe/dot_general | solution.py:59
  435.3 10.6 %while.62 = (s32[]{:T(128)}, f32[8,128,128]{2,1,0:T(8,128)S(1)}, f32[4,8,128,128]{3,2,1,0:T(8,128)S(1)}, f32[4,8,128,128]{3,2,1,0:T(8,128)}, f32[4]{0:T(128)S(1)}, /*index=5*/s32[]{:T(128)}, s32[]{:T(128)}, s32[]{:T(128)}) while((s32[]{:T(128)}, f32[8,128,128]{2,1,0:T(8,128)S(1)}, f32[4,8,128,128]{3,2,1,0:T(8,128)S(1)}, ...), condition=%wide.region_7.8_spmd.clone, body=%wide.region_6.7_spmd.clone.sunk | while | flops 524292 | bytes 2621580 | solution.py:85
  446.8 23.6 %fusion.2 = f32[1024,4096]{1,0:T(8,128)} fusion(bf16[2048,1024]{0,1:T(8,128)(2,1)} %bitcast.157, bf16[1,2048,4096]{2,1,0:T(8,128)(2,1)} %all-gather.6.cloned.1.call-done), kind=kOutput, calls=%fused_computation.10 | convolution fusion | flops 17179869184 | bytes 37748736 | tf_op jit(solution)/shard_map/dot_general | solution.py:155
  470.4 9.9 %bitcast_add_fusion.10 = f32[4,512,8,128]{3,1,2,0:T(8,128)S(1)} fusion(f32[4,8,512,128]{3,2,1,0:T(8,128)} %fusion.34, f32[4,512]{1,0:T(4,128)S(1)} %convert_element_type.133, f32[4,8,128,128]{3,2,1,0:T(8,128)} %copy-done.3, bf16[4,512,8,128]{1,0,3,2:T(4,128)(2,1)} %reshape_reshape.3), kind=kOutput, calls=%fused_computation.24 | convolution fusion | flops 3225419776 | bytes 23076864 | tf_op jit(solution)/shard_map/nthf,nhef->nthe/dot_general | solution.py:91
  480.3 8.1 %copy.179 = f32[4,512,8,128]{3,2,1,0:T(8,128)} copy(f32[4,512,8,128]{3,1,2,0:T(8,128)S(1)} %bitcast_add_fusion.10) | data formatting | bytes 16777216 | tf_op jit(solution)/shard_map/add | solution.py:91
  488.4 9.9 %copy.181 = f32[2048,8,128]{0,2,1:T(8,128)} copy(f32[2048,8,128]{2,1,0:T(8,128)} %bitcast.147) | data formatting | bytes 16777216 | tf_op jit(solution)/shard_map/reshape | solution.py:103
  498.2 10.8 %fusion.9 = bf16[2048,8,128]{0,2,1:T(8,128)(2,1)} fusion(f32[2048,8,128]{0,2,1:T(8,128)} %copy.181, f32[8,128,128]{2,1,0:T(8,128)S(1)} %get-tuple-element.364, bf16[2048,8,128]{0,2,1:T(8,128)(2,1)} %bitcast.150, f32[2048]{0:T(1024)S(1)} %get-tuple-element.507), kind=kOutput, calls=%fused_computation.23 | convolution fusion | flops 3227516928 | bytes 17309696 | tf_op jit(solution)/shard_map/thf,hef->the/dot_general | solution.py:141
  515.5 11.9 %fusion.35 = f32[4,8,512,128]{3,2,1,0:T(8,128)} fusion(bf16[4,8,512,512]{3,2,1,0:T(8,128)(2,1)} %multiply_convert_fusion.1, bf16[4,512,8,128]{1,3,2,0:T(8,128)(2,1)} %copy.184), kind=kOutput, calls=%fused_computation.63 | convolution fusion | flops 2147483648 | bytes 29360128 | tf_op jit(solution)/shard_map/nhts,nthe->nshe/dot_general | solution.py:60
  527.3 8.2 %bitcast_add_fusion.8 = f32[4,512,8,128]{3,1,2,0:T(8,128)S(1)} fusion(f32[4,8,512,128]{3,2,1,0:T(8,128)} %fusion.35, f32[4,512]{1,0:T(4,128)S(1)} %copy-done.6, f32[4,8,128,128]{3,2,1,0:T(8,128)S(1)} %get-tuple-element.365, bf16[4,512,8,128]{3,2,1,0:T(8,128)(2,1)} %bitcast.140), kind=kOutput, calls=%fused_computation.21 | convolution fusion | flops 3225419776 | bytes 23076864 | tf_op jit(solution)/shard_map/nshf,nhef->nshe/dot_general | solution.py:94
  535.5 8.1 %copy.188 = f32[4,512,8,128]{3,2,1,0:T(8,128)} copy(f32[4,512,8,128]{3,1,2,0:T(8,128)S(1)} %bitcast_add_fusion.8) | data formatting | bytes 16777216 | tf_op jit(solution)/shard_map/add | solution.py:94
  543.6 9.4 %copy.190 = f32[2048,8,128]{0,2,1:T(8,128)} copy(f32[2048,8,128]{2,1,0:T(8,128)} %bitcast.148) | data formatting | bytes 16777216 | tf_op jit(solution)/shard_map/reshape | solution.py:104
  553.1 7.7 %fusion.36 = f32[4,8,128,512]{2,3,1,0:T(8,128)} fusion(f32[4,8,128,128]{3,2,1,0:T(8,128)S(1)} %get-tuple-element.365, bf16[4,512,8,128]{1,3,2,0:T(8,128)(2,1)} %copy.175), kind=kOutput, calls=%fused_computation.64 | convolution fusion | flops 3221225472 | bytes 14680064 | tf_op jit(solution)/shard_map/nshe,nhef->nshf/dot_general | solution.py:97
  560.7 17.0 %add_bitcast_fusion = f32[4,512,8,128]{3,1,2,0:T(8,128)} fusion(f32[4,8,128,512]{2,3,1,0:T(8,128)} %fusion.36, f32[4,512]{1,0:T(4,128)S(1)} %copy-done.6, bf16[4,8,512,512]{3,2,1,0:T(8,128)(2,1)} %multiply_convert_fusion, bf16[4,512,8,128]{1,0,3,2:T(4,128)(2,1)} %reshape_reshape.3), kind=kOutput, calls=%fused_computation.25 | convolution fusion | flops 2151677952 | bytes 37756928 | tf_op jit(solution)/shard_map/nhts,nthe->nshe/dot_general | solution.py:63
  577.7 11.7 %copy.198 = f32[4,512,8,128]{3,2,1,0:T(8,128)} copy(f32[4,512,8,128]{3,1,2,0:T(8,128)} %add_bitcast_fusion) | data formatting | bytes 16777216 | tf_op jit(solution)/shard_map/add | solution.py:97
  589.4 9.4 %copy.201 = f32[2048,8,128]{0,2,1:T(8,128)} copy(f32[2048,8,128]{2,1,0:T(8,128)} %bitcast.149) | data formatting | bytes 16777216 | tf_op jit(solution)/shard_map/reshape | solution.py:105
  598.9 11.1 %while.63 = (s32[]{:T(128)}, f32[8,128,128]{2,1,0:T(8,128)S(1)}, s32[]{:T(128)}, f32[4,8,128,128]{3,2,1,0:T(8,128)}, f32[4]{0:T(128)S(1)}, /*index=5*/s32[]{:T(128)}, s32[]{:T(128)}, s32[]{:T(128)}, s32[]{:T(128)}, f32[1]{0:T(128)}) while((s32[]{:T(128)}, f32[8,128,128]{2,1,0:T(8,128)S(1)}, s32[]{:T(128)}, ...), condition=%wide.region_9.10_spmd.clone, body=%wide.region_8.9_spmd.clone.sunk | while | flops 524297 | bytes 1573071 | solution.py:26
  610.0 10.9 %fusion.8 = bf16[2048,8,128]{0,2,1:T(8,128)(2,1)} fusion(f32[2048,8,128]{0,2,1:T(8,128)} %copy.190, f32[8,128,128]{2,1,0:T(8,128)S(1)} %get-tuple-element.367, bf16[2048,8,128]{2,1,0:T(8,128)(2,1)} %bitcast.141, f32[2048]{0:T(1024)S(1)} %copy-done.7), kind=kOutput, calls=%fused_computation.20 | convolution fusion | flops 3227516928 | bytes 17309696 | tf_op jit(solution)/shard_map/thf,hef->the/dot_general | solution.py:144
  627.5 11.7 %fusion.7 = bf16[2048,8,128]{0,2,1:T(8,128)(2,1)} fusion(f32[2048,8,128]{0,2,1:T(8,128)} %copy.201, f32[8,128,128]{2,1,0:T(8,128)S(1)} %get-tuple-element.367, bf16[2048,8,128]{2,1,0:T(8,128)(2,1)} %bitcast.143, f32[2048]{0:T(1024)S(1)} %copy-done.7), kind=kOutput, calls=%fused_computation.18 | convolution fusion | flops 3227516928 | bytes 17309696 | tf_op jit(solution)/shard_map/the,hef->thf/dot_general | solution.py:147
  645.6 56.1 %all-reduce.3.cloned.1.call-done = f32[1024,4096]{1,0:T(8,128)} async-done(((f32[1024,4096]{1,0:T(8,128)}), f32[1024,4096]{1,0:T(8,128)}) %all-reduce.3.cloned.1.call-update) | async-done | bytes 16777232 | tf_op jit(solution)/shard_map/psum | solution.py:158
  (108 shorter events, 113.8 us)
Async XLA Ops:
  7.2 124.7 %all-gather.8.cloned.1.call-start = ((), (), s32[]{:S(2)}) async-start(), calls=%async_computation.2 | async-start | bytes 2621440 | tf_op jit(solution)/shard_map/all_gather | solution.py:13
  8.4 5.4 copy-start.5
  16.9 7.6 %copy-start.8 = (s32[1,7]{1,0:T(1,128)S(1)}, s32[1,7]{1,0:T(1,128)}, u32[]{:S(2)}) copy-start(s32[1,7]{1,0:T(1,128)} %param.19) | copy-start | bytes 88
  43.1 0.8 copy-start.1
  43.1 16.7 %copy-start.3 = (f32[4,8,128,128]{3,2,1,0:T(8,128)}, f32[4,8,128,128]{3,2,1,0:T(8,128)S(1)}, u32[]{:S(2)}) copy-start(f32[4,8,128,128]{3,2,1,0:T(8,128)S(1)} %get-tuple-element.362) | copy-start | bytes 6291460
  43.1 3.7 copy-start.11
  43.9 326.4 %all-gather.6.cloned.1.call-start = ((), (), s32[]{:S(2)}) async-start(), calls=%async_computation | async-start | bytes 20971520 | tf_op jit(solution)/shard_map/all_gather | solution.py:121
  44.6 554.2 %all-gather.10.cloned.1.call-start = ((), (), s32[]{:S(2)}) async-start(), calls=%async_computation.3 | async-start | bytes 2621440 | tf_op jit(solution)/shard_map/all_gather | solution.py:13
  86.8 17.2 %copy-start.4 = (f32[4,8,128,128]{3,2,1,0:T(8,128)S(1)}, f32[4,8,128,128]{3,2,1,0:T(8,128)}, u32[]{:S(2)}) copy-start(f32[4,8,128,128]{3,2,1,0:T(8,128)} %copy-done.3) | copy-start | bytes 6291460
  142.8 10.8 %copy-start.9 = (f32[4]{0:T(128)}, f32[4]{0:T(128)S(1)}, u32[]{:S(2)}) copy-start(f32[4]{0:T(128)S(1)} %get-tuple-element.750) | copy-start | bytes 52
  445.9 0.8 copy-start
  446.7 255.0 %all-reduce.3.cloned.1.call-start = ((), (), s32[]{:S(2)}) async-start(), calls=%async_computation.1 | async-start | bytes 33554432 | tf_op jit(solution)/shard_map/psum | solution.py:158
  515.5 11.9 %copy-start.6 = (f32[4,512]{1,0:T(4,128)S(1)}, f32[4,512]{1,0:T(4,128)}, u32[]{:S(2)}) copy-start(f32[4,512]{1,0:T(4,128)} %get-tuple-element.502) | copy-start | bytes 24580
  589.4 9.5 %copy-start.2 = (f32[8,128,128]{2,1,0:T(8,128)S(1)}, f32[8,128,128]{2,1,0:T(8,128)}, u32[]{:S(2)}) copy-start(f32[8,128,128]{2,1,0:T(8,128)} %custom-call.3) | copy-start | bytes 1572868
  589.4 9.5 %copy-start.10 = (f32[4]{0:T(128)S(1)}, f32[4]{0:T(128)}, u32[]{:S(2)}) copy-start(f32[4]{0:T(128)} %copy-done.9) | copy-start | bytes 52
  598.9 11.1 %copy-start.7 = (f32[2048]{0:T(1024)S(1)}, f32[2048]{0:T(1024)}, u32[]{:S(2)}) copy-start(f32[2048]{0:T(1024)} %get-tuple-element.506) | copy-start | bytes 24580
Sparse Core Ops, SparseCore 0:
  44.0 37.8 all-gather.7
  83.5 286.7 all-gather.5
  446.8 33.3 all-gather.9
  483.9 217.7 all-reduce.2
where the time goes:
time: 718 us; the launch traced here: 712 us
  waiting for transfers between devices  273 us (38%)
  matrix products  223 us (31%)
  local copies, waits for them, and re-layouts  147 us (20%)
  other arithmetic  34.7 us (5%)
  between operations  15.6 us (2%)
  blocking collectives  11.7 us (2%)
    all_gather x1, waiting for transfers between devices, on_device(): lax.all_gather(out_cotangent, 'head', axis=2, tiled=True)[0]  217 us
    psum x1, waiting for transfers between devices, on_device(): summed = lax.psum(partial_grad, ('seq', 'rep'))  56.1 us
    unnamed x33, local copies, waits for them, and re-layouts  36.1 us
    dot_general x1, matrix products, on_device(): lax.dot_general(full_cotangent, out_weight, (((1,), (1,)), ((), ())), pre...  24.1 us
    dot_general x1, matrix products, on_device(): lax.dot_general(attention_out, full_cotangent, (((0,), (0,)), ((), ())),...  23.6 us
    dot_general x1, matrix products, local_pass(): jnp.einsum('nhts,nshe->nthe', attn, value_blocks, preferred_element_type=...  17.2 us
    dot_general x1, matrix products, local_pass(): jnp.einsum('nhts,nthe->nshe', attn, grad_blocks, preferred_element_type=j...  17 us
    add x8, other arithmetic, link_step(): return (item[0] + item[1] * state, state)  15 us
  transfers between devices with their start and end apart: 4, of which 2 were waited for; matrix products, arithmetic and copies ran while one was open for 41% of the time, Pallas kernels for 0%

commit v1 on v0

--- a/solution.py
+++ b/solution.py
@@ -6,6 +6,28 @@
 HD = 128
 BLOCK = 512
 highest = lax.Precision.HIGHEST
+
+
+def in_order(blocks, dim):
+    shape = list(blocks.shape[1:])
+    shape[dim] *= blocks.shape[0]
+    return jnp.moveaxis(blocks, 0, dim).reshape(shape)
+
+
+def gather_around(x, axis, dim):
+    size = lax.axis_size(axis)
+    pairs = [(i, (i + 1) % size) for i in range(size)]
+    back = [(b, a) for a, b in pairs]
+    lower, upper = ([], [])
+    for step in range(size - 1):
+        if step % 2 == 0:
+            lower.append(lax.ppermute(lower[-1] if lower else x, axis, pairs))
+        else:
+            upper.append(lax.ppermute(upper[-1] if upper else x, axis, back))
+    blocks = jnp.stack([*lower[::-1], x, *upper])
+    shift = lax.axis_index(axis) - len(lower)
+    blocks = blocks[(jnp.arange(size) - shift) % size]
+    return in_order(blocks, dim)
 
 
 def prefix(shard, axis, combine, identity, reverse):
@@ -118,7 +140,7 @@
     queries = query_heads[0].reshape(length, heads, HD)
     keys = key_heads[0].reshape(length, heads, HD)
     values = value_heads[0].reshape(length, heads, HD)
-    full_cotangent = lax.all_gather(out_cotangent, "head", axis=2, tiled=True)[0]
+    full_cotangent = gather_around(out_cotangent, "head", 2)[0]
     grads_flat = lax.dot_general(
         full_cotangent, out_weight, (((1,), (1,)), ((), ())), preferred_element_type=jnp.float32
     ).astype(jnp.bfloat16)

time: 718 us -> 685 us (0.954)
  waiting for transfers between devices: 273 us -> 169 us
  local copies, waits for them, and re-layouts: 147 us -> 193 us
  other arithmetic: 34.7 us -> 58.6 us
    all_gather x1 -> x0, waiting for transfers between devices: 217 us -> none  [on_device(): lax.all_gather(out_cotangent, 'head', axis=2, tiled=True)[0]]
    ppermute x0 -> x3, waiting for transfers between devices: none -> 130 us  [the longest x2 106 us: gather_around(): lower.append(lax.ppermute(lower[-1] if lower else x, axis, pairs))]
    gather x0 -> x4, local copies, waits for them, and re-layouts: none -> 22.7 us  [gather_around(): blocks = blocks[(jnp.arange(size) - shift) % size]]
    transpose x0 -> x1, local copies, waits for them, and re-layouts: none -> 21.9 us  [in_order(): return jnp.moveaxis(blocks, 0, dim).reshape(shape)]
    psum x1, waiting for transfers between devices: 56.1 us -> 38.3 us  [on_device(): summed = lax.psum(partial_grad, ('seq', 'rep'))]
    transpose x0 -> x1, other arithmetic: none -> 13.6 us  [in_order(): return jnp.moveaxis(blocks, 0, dim).reshape(shape)]
    another operation x0 -> x1, other arithmetic: none -> 7.32 us  [gather_around(): blocks = jnp.stack([*lower[::-1], x, *upper])]
    unnamed x33 -> x47, local copies, waits for them, and re-layouts: 36.1 us -> 37.7 us
  transfers between devices with their start and end apart: 4 -> 6, of which waited for: 2 -> 4; matrix products, arithmetic and copies ran while one was open for 41% -> 50% of each run, Pallas kernels for 0% -> 0%
where the time goes in v1:
time: 685 us; the launch traced here: 675 us
  matrix products  218 us (32%)
  local copies, waits for them, and re-layouts  193 us (28%)
  waiting for transfers between devices  169 us (25%)
  other arithmetic  58.6 us (9%)
  between operations  15.4 us (2%)
  blocking collectives  9.88 us (1%)
    ppermute x2, waiting for transfers between devices, gather_around(): lower.append(lax.ppermute(lower[-1] if lower else x, axis, pairs))  106 us
    psum x1, waiting for transfers between devices, on_device(): summed = lax.psum(partial_grad, ('seq', 'rep'))  38.3 us
    unnamed x47, local copies, waits for them, and re-layouts  37.7 us
    ppermute x1, waiting for transfers between devices, gather_around(): upper.append(lax.ppermute(upper[-1] if upper else x, axis, back))  24.3 us
    dot_general x1, matrix products, on_device(): lax.dot_general(full_cotangent, out_weight, (((1,), (1,)), ((), ())), pre...  23.6 us
    dot_general x1, matrix products, on_device(): lax.dot_general(attention_out, full_cotangent, (((0,), (0,)), ((), ())),...  23.6 us
    gather x4, local copies, waits for them, and re-layouts, gather_around(): blocks = blocks[(jnp.arange(size) - shift) % size]  22.7 us
    transpose x1, local copies, waits for them, and re-layouts, in_order(): return jnp.moveaxis(blocks, 0, dim).reshape(shape)  21.9 us
  transfers between devices with their start and end apart: 6, of which 4 were waited for; matrix products, arithmetic and copies ran while one was open for 50% of the time, Pallas kernels for 0%

profile of v1, /device:TPU:0, one launch (start us, length us, event | category | flops | bytes accessed | tf_op | source)
XLA Modules:
  0.0 674.7 jit_solution(14015734682756212847)
XLA Ops:
  37.3 10.0 %while.60 = (s32[]{:T(128)}, f32[8,128,128]{2,1,0:T(8,128)S(1)}, f32[4,8,128,128]{3,2,1,0:T(8,128)S(1)}, f32[4,8,128,128]{3,2,1,0:T(8,128)}, f32[4]{0:T(128)S(1)}, /*index=5*/s32[]{:T(128)}, s32[]{:T(128)}) while((s32[]{:T(128)}, f32[8,128,128]{2,1,0:T(8,128)S(1)}, f32[4,8,128,128]{3,2,1,0:T(8,128)S(1)}, ...), condition=%wide.region_3.4_spmd.clone, body=%wide.region_2.3_spmd.clone.sunk | while | flops 524291 | bytes 2621552 | solution.py:106
  66.6 11.9 %multiply_convert_fusion = bf16[4,8,512,512]{3,2,1,0:T(8,128)(2,1)} fusion(f32[4,512,512]{2,1,0:T(8,128)} %and_convert_fusion, bf16[4,512,8,128]{1,3,2,0:T(8,128)(2,1)} %copy.190, bf16[4,512,8,128]{1,3,2,0:T(8,128)(2,1)} %copy.181), kind=kOutput, calls=%fused_computation.11 | convolution fusion | flops 2164260864 | bytes 29360128 | tf_op jit(solution)/shard_map/nthe,nshe->nhts/dot_general | solution.py:70
  78.5 9.9 %all-reduce = f32[4]{0:T(128)S(1)} all-reduce(f32[4]{0:T(128)S(1)} %dynamic-update-slice), channel_id=1, replica_groups=mesh['seq'=4,'head'=4,'rep'=2] {'seq'}, use_global_device_ids=true, to_apply=%add | all-reduce | flops 4 | bytes 32
  88.4 15.7 %collective-permute-done = bf16[1,2048,1024]{2,1,0:T(8,128)(2,1)} collective-permute-done((bf16[1,2048,1024]{2,1,0:T(8,128)(2,1)}, bf16[1,2048,1024]{2,1,0:T(8,128)(2,1)}, u32[]{:S(2)}, u32[]{:S(2)}) %collective-permute-start) | collective-permute-done | bytes 4194336 | tf_op jit(solution)/shard_map/ppermute | solution.py:24
  104.3 14.7 %fusion.17 = f32[4,8,512,128]{3,2,1,0:T(8,128)} fusion(bf16[4,8,512,512]{3,2,1,0:T(8,128)(2,1)} %multiply_convert_fusion, bf16[4,512,8,128]{3,2,1,0:T(8,128)(2,1)} %bitcast.153), kind=kOutput, calls=%fused_computation.43 | convolution fusion | flops 2147483648 | bytes 29360128 | tf_op jit(solution)/shard_map/nhts,nshe->nthe/dot_general | solution.py:78
  119.0 8.2 %bitcast_add_fusion.5 = f32[4,512,8,128]{3,1,2,0:T(8,128)S(1)} fusion(f32[4,8,512,128]{3,2,1,0:T(8,128)} %fusion.17, f32[4,512]{1,0:T(4,128)S(1)} %convert_element_type.133, f32[4,8,128,128]{3,2,1,0:T(8,128)S(1)} %get-tuple-element.362, bf16[4,512,8,128]{1,3,2,0:T(8,128)(2,1)} %copy.190), kind=kOutput, calls=%fused_computation.17 | convolution fusion | flops 3225419776 | bytes 23076864 | tf_op jit(solution)/shard_map/nthe,nhef->nthf/dot_general | solution.py:110
  127.2 8.1 %copy.212 = f32[4,512,8,128]{3,2,1,0:T(8,128)} copy(f32[4,512,8,128]{3,1,2,0:T(8,128)S(1)} %bitcast_add_fusion.5) | data formatting | bytes 16777216 | tf_op jit(solution)/shard_map/add | solution.py:110
  135.3 9.3 %copy.215 = f32[2048,8,128]{0,2,1:T(8,128)} copy(f32[2048,8,128]{2,1,0:T(8,128)} %bitcast.161) | data formatting | bytes 16777216 | tf_op jit(solution)/shard_map/reshape | solution.py:124
  146.4 11.2 %while.61 = (s32[]{:T(128)}, f32[8,128,128]{2,1,0:T(8,128)S(1)}, s32[]{:T(128)}, f32[4,8,128,128]{3,2,1,0:T(8,128)}, f32[4]{0:T(128)S(1)}, /*index=5*/s32[]{:T(128)}, f32[1]{0:T(128)}, s32[]{:T(128)}) while((s32[]{:T(128)}, f32[8,128,128]{2,1,0:T(8,128)S(1)}, s32[]{:T(128)}, f32[4,8,128,128]{3,2,1,0:T(8,128)}, f32[4]{0:T(128)S(1)}, ...), condition=%wide.region_5.6_spmd.clone, body=%wide.region_4.5_spmd.clone.sunk | while | flops 524293 | bytes 1573001 | solution.py:48
  157.6 10.9 %fusion.2 = bf16[2048,8,128]{0,2,1:T(8,128)(2,1)} fusion(f32[2048,8,128]{0,2,1:T(8,128)} %copy.215, f32[8,128,128]{2,1,0:T(8,128)S(1)} %get-tuple-element.364, bf16[2048,8,128]{2,1,0:T(8,128)(2,1)} %bitcast.160, f32[2048]{0:T(1024)S(1)} %get-tuple-element.509), kind=kOutput, calls=%fused_computation.16 | convolution fusion | flops 3227516928 | bytes 17309696 | tf_op jit(solution)/shard_map/the,hef->thf/dot_general | solution.py:160
  168.5 24.3 %collective-permute-done.2 = bf16[1,2048,1024]{2,1,0:T(8,128)(2,1)} collective-permute-done((bf16[1,2048,1024]{2,1,0:T(8,128)(2,1)}, bf16[1,2048,1024]{2,1,0:T(8,128)(2,1)}, u32[]{:S(2)}, u32[]{:S(2)}) %collective-permute-start.2) | collective-permute-done | bytes 4194336 | tf_op jit(solution)/shard_map/ppermute | solution.py:26
  192.8 90.3 %collective-permute-done.1 = bf16[1,2048,1024]{2,1,0:T(8,128)(2,1)} collective-permute-done((bf16[1,2048,1024]{2,1,0:T(8,128)(2,1)}, bf16[1,2048,1024]{2,1,0:T(8,128)(2,1)}, u32[]{:S(2)}, u32[]{:S(2)}) %collective-permute-start.1) | collective-permute-done | bytes 4194336 | tf_op jit(solution)/shard_map/ppermute | solution.py:24
  316.6 13.6 %maximum_bitcast_fusion = bf16[1,2048,4,1024]{3,1,2,0:T(8,128)(2,1)} fusion(bf16[4,1,512,1024]{3,2,0,1:T(8,128)(2,1)} %bitcast.175, bf16[4,1,768,1024]{3,2,0,1:T(8,128)(2,1)} %bitcast.166, bf16[4,1,768,1024]{3,2,0,1:T(8,128)(2,1)} %bitcast.165), kind=kLoop, calls=%fused_computation.14 | loop fusion | flops 50331648 | bytes 33554432 | tf_op jit(solution)/shard_map/transpose | solution.py:14
  330.3 21.9 %copy.177 = bf16[1,2048,4,1024]{1,3,2,0:T(8,128)(2,1)} copy(bf16[1,2048,4,1024]{3,1,2,0:T(8,128)(2,1)} %maximum_bitcast_fusion) | data formatting | bytes 33554432 | tf_op jit(solution)/shard_map/transpose | solution.py:14
  352.2 23.6 %convolution_convert_fusion = bf16[2048,1024]{0,1:T(8,128)(2,1)} fusion(bf16[1024,4096]{1,0:T(8,128)(2,1)} %param.18, bf16[2048,4096]{0,1:T(8,128)(2,1)} %bitcast.167), kind=kOutput, calls=%fused_computation.38 | convolution fusion | flops 17181966336 | bytes 29360128 | tf_op jit(solution)/shard_map/dot_general | solution.py:144
  375.8 8.2 %reshape_reshape.3 = bf16[4,512,8,128]{1,0,3,2:T(4,128)(2,1)} reshape(bf16[2048,1024]{0,1:T(8,128)(2,1)} %convolution_convert_fusion) | data formatting | bytes 8388608 | tf_op jit(solution)/shard_map/reshape;reshape | solution.py:61
  390.7 9.5 %while.62 = (s32[]{:T(128)}, f32[8,128,128]{2,1,0:T(8,128)S(1)}, f32[4,8,128,128]{3,2,1,0:T(8,128)S(1)}, f32[4,8,128,128]{3,2,1,0:T(8,128)}, f32[4]{0:T(128)S(1)}, /*index=5*/s32[]{:T(128)}, s32[]{:T(128)}, s32[]{:T(128)}) while((s32[]{:T(128)}, f32[8,128,128]{2,1,0:T(8,128)S(1)}, f32[4,8,128,128]{3,2,1,0:T(8,128)S(1)}, ...), condition=%wide.region_7.8_spmd.clone, body=%wide.region_6.7_spmd.clone.sunk | while | flops 524292 | bytes 2621572 | solution.py:107
  408.3 16.4 %add_bitcast_fusion = f32[4,512,8,128]{3,1,2,0:T(8,128)} fusion(f32[4,8,128,512]{2,3,1,0:T(8,128)} %fusion.31, f32[4,512]{1,0:T(4,128)S(1)} %copy-done.12, bf16[4,8,512,512]{3,2,1,0:T(8,128)(2,1)} %multiply_convert_fusion, bf16[4,512,8,128]{1,0,3,2:T(4,128)(2,1)} %reshape_reshape.3), kind=kOutput, calls=%fused_computation.26 | convolution fusion | flops 2151677952 | bytes 37756928 | tf_op jit(solution)/shard_map/nhts,nthe->nshe/dot_general | solution.py:85
  424.7 23.6 %fusion.32 = f32[1024,4096]{1,0:T(8,128)} fusion(bf16[2048,1024]{0,1:T(8,128)(2,1)} %bitcast.179, bf16[2048,4096]{0,1:T(8,128)(2,1)} %bitcast.168), kind=kOutput, calls=%fused_computation.76 | convolution fusion | flops 17179869184 | bytes 37748736 | tf_op jit(solution)/shard_map/dot_general | solution.py:177
  448.3 12.0 %multiply_convert_fusion.1 = bf16[4,8,512,512]{3,2,1,0:T(8,128)(2,1)} fusion(f32[4,512,512]{2,1,0:T(8,128)} %and_convert_fusion, bf16[4,512,8,128]{1,0,3,2:T(4,128)(2,1)} %reshape_reshape.3, bf16[4,512,8,128]{3,2,1,0:T(8,128)(2,1)} %bitcast.154), kind=kOutput, calls=%fused_computation.12 | convolution fusion | flops 2164260864 | bytes 29360128 | tf_op jit(solution)/shard_map/nthe,nshe->nhts/dot_general | solution.py:74
  460.2 11.6 %copy.204 = f32[4,512,8,128]{3,2,1,0:T(8,128)} copy(f32[4,512,8,128]{3,1,2,0:T(8,128)} %add_bitcast_fusion) | data formatting | bytes 16777216 | tf_op jit(solution)/shard_map/add | solution.py:119
  471.8 9.6 %copy.207 = f32[2048,8,128]{0,2,1:T(8,128)} copy(f32[2048,8,128]{2,1,0:T(8,128)} %bitcast.162) | data formatting | bytes 16777216 | tf_op jit(solution)/shard_map/reshape | solution.py:127
  481.5 11.7 %fusion.30 = f32[4,8,512,128]{3,2,1,0:T(8,128)} fusion(bf16[4,8,512,512]{3,2,1,0:T(8,128)(2,1)} %multiply_convert_fusion.1, bf16[4,512,8,128]{1,3,2,0:T(8,128)(2,1)} %copy.190), kind=kOutput, calls=%fused_computation.74 | convolution fusion | flops 2147483648 | bytes 29360128 | tf_op jit(solution)/shard_map/nhts,nthe->nshe/dot_general | solution.py:82
  509.2 9.4 %copy.196 = f32[2048,8,128]{0,2,1:T(8,128)} copy(f32[2048,8,128]{2,1,0:T(8,128)} %bitcast.163) | data formatting | bytes 16777216 | tf_op jit(solution)/shard_map/reshape | solution.py:126
  518.6 15.2 %fusion.29 = f32[4,8,512,128]{3,2,1,0:T(8,128)} fusion(bf16[4,8,512,512]{3,2,1,0:T(8,128)(2,1)} %multiply_convert_fusion.1, bf16[4,512,8,128]{1,3,2,0:T(8,128)(2,1)} %copy.181), kind=kOutput, calls=%fused_computation.73 | convolution fusion | flops 2147483648 | bytes 29360128 | tf_op jit(solution)/shard_map/nhts,nshe->nthe/dot_general | solution.py:81
  533.9 10.7 %bitcast_add_fusion.10 = f32[4,512,8,128]{3,1,2,0:T(8,128)S(1)} fusion(f32[4,8,512,128]{3,2,1,0:T(8,128)} %fusion.29, f32[4,512]{1,0:T(4,128)S(1)} %copy-done.11, f32[4,8,128,128]{3,2,1,0:T(8,128)S(1)} %copy-done.8, bf16[4,512,8,128]{1,0,3,2:T(4,128)(2,1)} %reshape_reshape.3), kind=kOutput, calls=%fused_computation.25 | convolution fusion | flops 3225419776 | bytes 23076864 | tf_op jit(solution)/shard_map/nthf,nhef->nthe/dot_general | solution.py:113
  552.7 9.6 %copy.187 = f32[2048,8,128]{0,2,1:T(8,128)} copy(f32[2048,8,128]{2,1,0:T(8,128)} %bitcast.164) | data formatting | bytes 16777216 | tf_op jit(solution)/shard_map/reshape | solution.py:125
  562.3 11.1 %fusion.5 = bf16[2048,8,128]{0,2,1:T(8,128)(2,1)} fusion(f32[2048,8,128]{0,2,1:T(8,128)} %copy.187, f32[8,128,128]{2,1,0:T(8,128)S(1)} %copy-done.6, bf16[2048,8,128]{0,2,1:T(8,128)(2,1)} %bitcast.169, f32[2048]{0:T(1024)S(1)} %copy-done.15), kind=kOutput, calls=%fused_computation.24 | convolution fusion | flops 3227516928 | bytes 17309696 | tf_op jit(solution)/shard_map/thf,hef->the/dot_general | solution.py:163
  579.9 11.0 %while.63 = (s32[]{:T(128)}, f32[8,128,128]{2,1,0:T(8,128)S(1)}, s32[]{:T(128)}, f32[4,8,128,128]{3,2,1,0:T(8,128)}, f32[4]{0:T(128)S(1)}, /*index=5*/s32[]{:T(128)}, s32[]{:T(128)}, s32[]{:T(128)}, s32[]{:T(128)}, f32[1]{0:T(128)}) while((s32[]{:T(128)}, f32[8,128,128]{2,1,0:T(8,128)S(1)}, s32[]{:T(128)}, ...), condition=%wide.region_9.10_spmd.clone, body=%wide.region_8.9_spmd.clone.sunk | while | flops 524297 | bytes 1573063 | solution.py:48
  590.9 11.8 %fusion.3 = bf16[2048,8,128]{0,2,1:T(8,128)(2,1)} fusion(f32[2048,8,128]{0,2,1:T(8,128)} %copy.207, f32[8,128,128]{2,1,0:T(8,128)S(1)} %get-tuple-element.367, bf16[2048,8,128]{2,1,0:T(8,128)(2,1)} %bitcast.158, f32[2048]{0:T(1024)S(1)} %copy-done.13), kind=kOutput, calls=%fused_computation.19 | convolution fusion | flops 3227516928 | bytes 17309696 | tf_op jit(solution)/shard_map/the,hef->thf/dot_general | solution.py:169
  609.3 10.8 %fusion.4 = bf16[2048,8,128]{0,2,1:T(8,128)(2,1)} fusion(f32[2048,8,128]{0,2,1:T(8,128)} %copy.196, f32[8,128,128]{2,1,0:T(8,128)S(1)} %get-tuple-element.367, bf16[2048,8,128]{2,1,0:T(8,128)(2,1)} %bitcast.156, f32[2048]{0:T(1024)S(1)} %copy-done.13), kind=kOutput, calls=%fused_computation.21 | convolution fusion | flops 3227516928 | bytes 17309696 | tf_op jit(solution)/shard_map/thf,hef->the/dot_general | solution.py:166
  626.5 38.3 %all-reduce.3.cloned.1.call-done = f32[1024,4096]{1,0:T(8,128)} async-done(((f32[1024,4096]{1,0:T(8,128)}), f32[1024,4096]{1,0:T(8,128)}) %all-reduce.3.cloned.1.call-update) | async-done | bytes 16777232 | tf_op jit(solution)/shard_map/psum | solution.py:180
  (135 shorter events, 180.9 us)
Async XLA Ops:
  7.2 139.2 %all-gather.5.cloned.1.call-start = ((), (), s32[]{:S(2)}) async-start(), calls=%async_computation.1 | async-start | bytes 2621440 | tf_op jit(solution)/shard_map/all_gather | solution.py:35
  7.2 96.9 %collective-permute-start = (bf16[1,2048,1024]{2,1,0:T(8,128)(2,1)}, bf16[1,2048,1024]{2,1,0:T(8,128)(2,1)}, u32[]{:S(2)}, u32[]{:S(2)}) collective-permute-start(bf16[1,2048,1024]{2,1,0:T(8,128)(2,1)} %param.17), channel_id=1, source_target_pairs={{0,2},{2,4},{4,6},{6,0},{1,3},{3,5},{5,7},{7,1},{8,10},{10,12},{12... | collective-permute-start | bytes 12582920 | tf_op jit(solution)/shard_map/ppermute | solution.py:24
  10.3 182.5 %collective-permute-start.2 = (bf16[1,2048,1024]{2,1,0:T(8,128)(2,1)}, bf16[1,2048,1024]{2,1,0:T(8,128)(2,1)}, u32[]{:S(2)}, u32[]{:S(2)}) collective-permute-start(bf16[1,2048,1024]{2,1,0:T(8,128)(2,1)} %param.17), channel_id=1, source_target_pairs={{2,0},{4,2},{6,4},{0,6},{3,1},{5,3},{7,5},{1,7},{10,8},{12,10},{14... | collective-permute-start | bytes 12582920 | tf_op jit(solution)/shard_map/ppermute | solution.py:26
  28.9 5.5 copy-start.1
  32.4 2.0 copy-start
  47.3 0.8 copy-start.3
  47.4 71.7 %copy-start.7 = (f32[4,8,128,128]{3,2,1,0:T(8,128)}, f32[4,8,128,128]{3,2,1,0:T(8,128)S(1)}, u32[]{:S(2)}) copy-start(f32[4,8,128,128]{3,2,1,0:T(8,128)S(1)} %get-tuple-element.362) | copy-start | bytes 6291460
  48.2 531.7 %all-gather.7.cloned.1.call-start = ((), (), s32[]{:S(2)}) async-start(), calls=%async_computation.2 | async-start | bytes 2621440 | tf_op jit(solution)/shard_map/all_gather | solution.py:35
  54.1 8.7 %copy-start.18 = (u32[32]{0:T(128)S(1)}, u32[32]{0:T(128)}, u32[]{:S(2)}) copy-start(u32[32]{0:T(128)} %constant.177) | copy-start | bytes 388
  88.4 30.6 %copy-start.10 = (f32[4,512]{1,0:T(4,128)}, f32[4,512]{1,0:T(4,128)S(1)}, u32[]{:S(2)}) copy-start(f32[4,512]{1,0:T(4,128)S(1)} %convert_element_type.133) | copy-start | bytes 24580
  104.1 178.9 %collective-permute-start.1 = (bf16[1,2048,1024]{2,1,0:T(8,128)(2,1)}, bf16[1,2048,1024]{2,1,0:T(8,128)(2,1)}, u32[]{:S(2)}, u32[]{:S(2)}) collective-permute-start(bf16[1,2048,1024]{2,1,0:T(8,128)(2,1)} %collective-permute-done), channel_id=1, source_target_pairs={{0,2},{2,4},{4,6},{6,0},{1,3},{3,5},{5,7},{7,1},{8,10},{10,12},{12... | collective-permute-start | bytes 12582920 | tf_op jit(solution)/shard_map/ppermute | solution.py:24
  146.4 22.1 %copy-start.14 = (f32[2048]{0:T(1024)}, f32[2048]{0:T(1024)S(1)}, u32[]{:S(2)}) copy-start(f32[2048]{0:T(1024)S(1)} %get-tuple-element.509) | copy-start | bytes 24580
  157.5 10.9 %copy-start.5 = (f32[8,128,128]{2,1,0:T(8,128)}, f32[8,128,128]{2,1,0:T(8,128)S(1)}, u32[]{:S(2)}) copy-start(f32[8,128,128]{2,1,0:T(8,128)S(1)} %get-tuple-element.364) | copy-start | bytes 1572868
  157.5 10.9 %copy-start.16 = (f32[4]{0:T(128)}, f32[4]{0:T(128)S(1)}, u32[]{:S(2)}) copy-start(f32[4]{0:T(128)S(1)} %get-tuple-element.750) | copy-start | bytes 52
  157.6 125.5 %copy-start.9 = (bf16[1,2048,1024]{2,1,0:T(8,128)(2,1)S(1)}, bf16[1,2048,1024]{2,1,0:T(8,128)(2,1)}, u32[]{:S(2)}) copy-start(bf16[1,2048,1024]{2,1,0:T(8,128)(2,1)} %param.17) | copy-start | bytes 12582916
  400.3 7.9 %copy-start.2 = (f32[8,128,128]{2,1,0:T(8,128)}, f32[8,128,128]{2,1,0:T(8,128)S(1)}, u32[]{:S(2)}) copy-start(f32[8,128,128]{2,1,0:T(8,128)S(1)} %get-tuple-element.366) | copy-start | bytes 1572868
  400.3 8.0 %copy-start.12 = (f32[4,512]{1,0:T(4,128)S(1)}, f32[4,512]{1,0:T(4,128)}, u32[]{:S(2)}) copy-start(f32[4,512]{1,0:T(4,128)} %get-tuple-element.502) | copy-start | bytes 24580
  408.2 256.7 %all-reduce.3.cloned.1.call-start = ((), (), s32[]{:S(2)}) async-start(), calls=%async_computation | async-start | bytes 33554432 | tf_op jit(solution)/shard_map/psum | solution.py:180
  518.6 15.2 %copy-start.8 = (f32[4,8,128,128]{3,2,1,0:T(8,128)S(1)}, f32[4,8,128,128]{3,2,1,0:T(8,128)}, u32[]{:S(2)}) copy-start(f32[4,8,128,128]{3,2,1,0:T(8,128)} %copy-done.7) | copy-start | bytes 6291460
  518.6 15.2 %copy-start.11 = (f32[4,512]{1,0:T(4,128)S(1)}, f32[4,512]{1,0:T(4,128)}, u32[]{:S(2)}) copy-start(f32[4,512]{1,0:T(4,128)} %copy-done.10) | copy-start | bytes 24580
  552.7 9.6 %copy-start.6 = (f32[8,128,128]{2,1,0:T(8,128)S(1)}, f32[8,128,128]{2,1,0:T(8,128)}, u32[]{:S(2)}) copy-start(f32[8,128,128]{2,1,0:T(8,128)} %copy-done.5) | copy-start | bytes 1572868
  552.7 9.6 %copy-start.15 = (f32[2048]{0:T(1024)S(1)}, f32[2048]{0:T(1024)}, u32[]{:S(2)}) copy-start(f32[2048]{0:T(1024)} %copy-done.14) | copy-start | bytes 24580
  573.4 6.5 copy-start.4
  573.4 6.5 copy-start.17
  579.9 11.0 %copy-start.13 = (f32[2048]{0:T(1024)S(1)}, f32[2048]{0:T(1024)}, u32[]{:S(2)}) copy-start(f32[2048]{0:T(1024)} %get-tuple-element.508) | copy-start | bytes 24580
Sparse Core Ops, SparseCore 0:
  48.3 34.8 all-gather.4
  408.3 34.5 all-gather.6
  448.4 216.4 all-reduce.2
